TPU v7x, 32 devices: a whole 2x2x4 slice. The times are simulated.
32 devices in a mesh: wide: 16 (over z, y, core), narrow: 2 (over x).
Axes of the slice: x: 2, y: 2, z: 4, core: 2. Of those that a mesh axis runs over, the one named last changes fastest.
Arguments:
- concentrations: float32 [256, 32, 256], P('wide', 'narrow'), may hold values from 0.1 to 2
- wind_speeds: bfloat16 [2, 2, 32, 256], P(None, None, ('narrow', 'wide')), may hold values from -0.59765625 to 0.59765625
- rate_constants: float32 [768], replicated, may hold values from 0.05 to 1
- reactants: int32 [768, 2], replicated, may hold values from 0 to 255
- products: int32 [768, 2], replicated, may hold values from 0 to 255
Outputs:
- after_chemistry: float32 [256, 32, 256], P(None, ('narrow', 'wide'))
Inputs may be any that keep to these rules, and one draw needn't show every extreme that they name: `reactants`: each entry is a species number. `products`: each entry is a species number.
All inputs are finite; a program needn't handle non-finite values.
Results may differ from a plain program's by a relative error of at most 0.0003.
Values may be sent and summed in bfloat16 or wider, within the bound.
A program may use at most 64 MiB of HBM per device.

v0:
```python
import jax
import jax.numpy as jnp
from jax import lax
from jax.sharding import PartitionSpec as P

S = 256
SUB = 2
SECTIONS = 6


DIFFUSION = 0.1
CHEM_STEP = 0.02


def padded(cells, sides, width):
    for axis, dim in sides:
        count = lax.axis_size(axis)
        head = lax.slice_in_dim(cells, 0, width, axis=dim)
        tail = lax.slice_in_dim(cells, cells.shape[dim] - width, cells.shape[dim], axis=dim)
        cells = jnp.concatenate(
            [
                lax.ppermute(tail, axis, [(i, (i + 1) % count) for i in range(count)]),
                cells,
                lax.ppermute(head, axis, [((i + 1) % count, i) for i in range(count)]),
            ],
            axis=dim,
        )
    return cells


def take_range(array, begin_at, end_at, along):
    along = along % array.ndim
    index = [slice(None)] * array.ndim
    index[along] = slice(begin_at, end_at)
    return array[tuple(index)]


def minmod(first_jump, second_jump):
    return jnp.maximum(0.0, jnp.minimum(first_jump, second_jump)) + jnp.minimum(
        0.0, jnp.maximum(first_jump, second_jump)
    )


def sweep_axis(extended, speeds, along, closed):
    length = extended.shape[along]
    speed_face = 0.5 * (
        take_range(speeds, 0, length - 1, along) + take_range(speeds, 1, length, along)
    )
    jumps = take_range(extended, 1, length, along) - take_range(extended, 0, length - 1, along)
    slopes = minmod(
        take_range(jumps, 0, length - 2, along), take_range(jumps, 1, length - 1, along)
    )
    inner_speed = take_range(speed_face, 1, length - 2, along)
    left_value = take_range(extended, 1, length - 2, along) + 0.5 * (
        1.0 - inner_speed
    ) * take_range(slopes, 0, length - 3, along)
    right_value = take_range(extended, 2, length - 1, along) - 0.5 * (
        1.0 + inner_speed
    ) * take_range(slopes, 1, length - 2, along)
    face_flux = inner_speed * jnp.where(
        inner_speed >= 0.0, left_value, right_value
    ) - DIFFUSION * take_range(jumps, 1, length - 2, along)
    if closed:
        position = lax.broadcasted_iota(jnp.int32, face_flux.shape, along % face_flux.ndim)
        face_flux = jnp.where((position > 0) & (position < length - 4), face_flux, 0.0)
    return take_range(extended, 2, length - 2, along) - (
        take_range(face_flux, 1, length - 3, along) - take_range(face_flux, 0, length - 4, along)
    )


def sweep_second(tracer, speeds):
    pad_tracer = [(0, 0)] * (tracer.ndim - 1) + [(2, 2)]
    pad_speeds = [(0, 0)] * (speeds.ndim - 1) + [(2, 2)]
    return sweep_axis(
        jnp.pad(tracer, pad_tracer, mode="edge"), jnp.pad(speeds, pad_speeds, mode="edge"), -1, True
    )


def react_cells(cell_block, rate_constants, first_ids, second_ids, net_matrix):
    for section_index in range(SECTIONS):
        rate_values = (
            rate_constants[:, None]
            * jnp.take(cell_block, first_ids, axis=0)
            * jnp.take(cell_block, second_ids, axis=0)
        )
        cell_block = cell_block + CHEM_STEP * jnp.dot(
            net_matrix, rate_values, precision=lax.Precision.HIGHEST
        )
    return cell_block


def on_device(concentrations, wind_speeds, rate_constants, reactants, products):
    groups = concentrations.shape[0]
    row_count = wind_speeds.shape[2]
    columns = wind_speeds.shape[3]
    wide_count = lax.axis_size("wide")
    planes = wind_speeds.reshape(SUB * 2, row_count, columns)
    gathered = lax.all_gather(planes, "wide", axis=1, tiled=True).astype(jnp.float32)
    tracer = concentrations
    stacked = jnp.concatenate([tracer, gathered], 0)
    extended = padded(stacked, (("narrow", 1),), 4)
    wind_rims = extended[groups:]
    tracer = sweep_axis(extended[:groups], wind_rims[0], -2, False)
    tracer = sweep_second(tracer, wind_rims[1, 2:-2])
    tracer = sweep_axis(tracer, wind_rims[2, 2:-2], -2, False)
    tracer = sweep_second(tracer, wind_rims[3, 4:-4])
    species_ids = lax.broadcasted_iota(jnp.int32, (S, rate_constants.shape[0]), 0)

    def one_hot(species_column):
        return (species_ids == species_column[None, :]).astype(jnp.float32)

    net_matrix = (
        one_hot(products[:, 0])
        + one_hot(products[:, 1])
        - one_hot(reactants[:, 0])
        - one_hot(reactants[:, 1])
    )
    first_ids = reactants[:, 0]
    second_ids = reactants[:, 1]
    shaped = tracer.reshape(groups, wide_count, row_count, columns)
    cell_block = lax.all_to_all(shaped, "wide", split_axis=1, concat_axis=0, tiled=True)
    flattened = cell_block.reshape(cell_block.shape[0], -1)
    regrouped = react_cells(flattened, rate_constants, first_ids, second_ids, net_matrix).reshape(
        cell_block.shape
    )
    return regrouped.reshape(S, row_count, columns)


def solution(mesh):
    return jax.shard_map(
        on_device,
        mesh=mesh,
        in_specs=(
            P("wide", "narrow", None),
            P(None, None, ("narrow", "wide"), None),
            P(),
            P(),
            P(),
        ),
        out_specs=P(None, ("narrow", "wide"), None),
        check_vma=False,
    )
```

profile of v0, /device:TPU:0, one launch (start us, length us, event | category | flops | bytes accessed | tf_op | source)
XLA Modules:
  0.0 136.4 jit_solution(5072353564964290958)
XLA Ops:
  0.0 0.7 reshape.84
  0.7 23.2 %all_gather.3 = bf16[4,16,256]{2,0,1:T(4,128)(2,1)S(1)} all-gather(bf16[4,1,256]{2,0,1:T(4,128)(2,1)S(1)} %reshape.84), channel_id=1, replica_groups=mesh['wide'=16,'narrow'=2] {'wide'}, dimensions={1}, use_global_device_ids=true | all-gather | bytes 34816 | tf_op jit(solution)/shard_map/all_gather | solution.py:98
  23.9 1.0 constant_dynamic-update-slice_fusion
  24.9 1.6 %collective-permute-start = (f32[20,4,256]{2,1,0:T(4,128)S(1)}, f32[20,4,256]{2,1,0:T(4,128)S(1)}, u32[]{:S(2)}, u32[]{:S(2)}) collective-permute-start(f32[20,4,256]{2,1,0:T(4,128)S(1)} %get-tuple-element.30), channel_id=1, source_target_pairs={{0,1},{1,0},{2,3},{3,2},{4,5},{5,4},{6,7},{7,6},{8,9},{9,8},{10,11... | collective-permute-start | bytes 245768 | tf_op jit(solution)/shard_map/ppermute | solution.py:22
  26.5 0.5 collective-permute-start.1
  27.8 0.8 copy.82
  28.6 0.7 copy.80
  29.3 0.8 slice_reduce_fusion.5
  30.1 0.6 compare_select_fusion
  30.7 0.6 fusion.90
  31.6 0.6 broadcast_compare_fusion.3
  32.2 0.6 subtract_multiply_fusion.3
  32.9 0.8 copy.63
  34.2 0.7 broadcast_compare_fusion
  34.9 0.6 subtract_multiply_fusion
  35.5 0.8 copy.71
  36.3 0.6 broadcast_compare_fusion.2
  36.9 0.6 subtract_multiply_fusion.2
  37.5 0.8 copy.75
  38.3 2.5 %copy.88 = f32[16,23,256]{1,0,2:T(8,128)} copy(f32[16,23,256]{2,1,0:T(8,128)S(1)} %get-tuple-element.29) | data formatting | bytes 753664
  40.8 2.5 %copy.89 = f32[16,23,256]{1,0,2:T(8,128)} copy(f32[16,23,256]{2,1,0:T(8,128)S(1)} %get-tuple-element.28) | data formatting | bytes 753664
  43.2 2.5 %sub.79 = f32[16,23,256]{1,0,2:T(8,128)S(1)} subtract(f32[16,23,256]{1,0,2:T(8,128)} %copy.88, f32[16,23,256]{1,0,2:T(8,128)} %copy.89) | non-fusion elementwise | flops 94208 | bytes 1130496 | tf_op jit(solution)/shard_map/sub | solution.py:49
  45.7 1.9 %minimum_add_fusion.3 = f32[16,22,256]{1,0,2:T(8,128)} fusion(f32[16,23,256]{1,0,2:T(8,128)S(1)} %sub.79), kind=kLoop, calls=%fused_computation.67 | loop fusion | flops 450560 | bytes 1081344 | tf_op jit(solution)/shard_map/add | solution.py:39
  47.6 2.5 %copy.87 = f32[16,21,256]{1,0,2:T(8,128)} copy(f32[16,21,256]{2,1,0:T(8,128)S(1)} %get-tuple-element.26) | data formatting | bytes 688128
  50.1 2.5 %copy.90 = f32[16,21,256]{1,0,2:T(8,128)} copy(f32[16,21,256]{2,1,0:T(8,128)S(1)} %get-tuple-element.27) | data formatting | bytes 688128
  52.7 0.8 copy.70
  53.6 0.8 copy.64
  54.4 2.5 %copy.86 = f32[16,20,256]{1,0,2:T(8,128)} copy(f32[16,20,256]{2,1,0:T(8,128)S(1)} %slice.393) | data formatting | bytes 655360
  56.9 4.8 %fusion.22 = f32[16,21,256]{1,0,2:T(8,128)S(1)} fusion(f32[16,23,256]{1,0,2:T(8,128)S(1)} %sub.79, f32[16,21,256]{1,0,2:T(8,128)} %copy.90, f32[16,22,256]{1,0,2:T(8,128)} %minimum_add_fusion.3, f32[16,21,256]{1,0,2:T(8,128)} %copy.87, f32[21,256]{0,1:T(8,128)S(1)} %copy.70, f32[21,256]{0,1:T(8,128)S(1)} %copy.66, f32[21,256]{0,1:T(8,128)S(1)} %copy-done.7, ...), kind=kLoop, calls=%fused_computation.59 | loop fusion | flops 688128 | bytes 2134272 | tf_op jit(solution)/shard_map/sub | solution.py:60
  61.7 0.6 fusion.21
  62.5 1.1 copy-done
  63.8 1.7 %minimum_add_fusion.1 = f32[16,20,258]{1,0,2:T(8,128)} fusion(f32[16,20,259]{1,0,2:T(8,128)S(1)} %slice_subtract_fusion.1), kind=kLoop, calls=%fused_computation.17 | loop fusion | flops 412800 | bytes 990720 | tf_op jit(solution)/shard_map/add | solution.py:39
  65.9 6.3 %fusion.7 = f32[16,20,257]{1,0,2:T(8,128)S(1)} fusion(f32[16,20,259]{1,0,2:T(8,128)S(1)} %slice_subtract_fusion.1, f32[16,20,258]{1,0,2:T(8,128)} %minimum_add_fusion.1, f32[16,20,2]{1,0,2:T(8,128)S(1)} %reshape.88, f32[16,20,256]{1,0,2:T(8,128)} %copy-done, f32[16,20,2]{1,0,2:T(8,128)S(1)} %reshape.87, f32[20,257]{0,1:T(8,128)S(1)} %copy.74, ...), kind=kLoop, calls=%fused_computation.31 | loop fusion | flops 904640 | bytes 1715717 | tf_op jit(solution)/shard_map/jit(_where)/select_n | solution.py:65
  72.3 0.3 fusion.20
  72.5 0.6 slice_subtract_fusion.4
  73.2 1.9 %minimum_add_fusion.2 = f32[16,18,256]{1,0,2:T(8,128)} fusion(f32[16,19,256]{1,0,2:T(8,128)S(1)} %slice_subtract_fusion.4), kind=kLoop, calls=%fused_computation.66 | loop fusion | flops 368640 | bytes 884736 | tf_op jit(solution)/shard_map/add | solution.py:39
  75.5 5.1 %fusion.15 = f32[16,17,256]{1,0,2:T(8,128)S(1)} fusion(f32[16,19,256]{1,0,2:T(8,128)} %copy-done.2, f32[16,18,256]{1,0,2:T(8,128)} %minimum_add_fusion.2, f32[16,20,256]{1,0,2:T(8,128)S(1)} %fusion.20, f32[17,256]{0,1:T(8,128)S(1)} %copy.78, f32[17,256]{0,1:T(8,128)S(1)} %copy.77, f32[17,256]{0,1:T(8,128)S(1)} %copy-done.6, pred[17,256]{0,1:T(8,128)(4,1)S(1)} %copy.76), kind=kLoop, calls=%fused_computation.46 | loop fusion | flops 557056 | bytes 1727744 | tf_op jit(solution)/shard_map/sub | solution.py:60
  80.6 1.1 fusion.14
  82.1 0.3 minimum_add_fusion
  82.4 0.5 copy-done.4
  83.0 2.8 %fusion.1 = f32[16,16,257]{1,0,2:T(8,128)S(1)} fusion(f32[16,16,259]{1,0,2:T(8,128)S(1)} %slice_subtract_fusion, f32[16,16,258]{1,0,2:T(8,128)S(1)} %minimum_add_fusion, f32[16,16,2]{1,0,2:T(8,128)S(1)} %reshape.92, f32[16,16,256]{1,0,2:T(8,128)S(1)} %fusion.14, f32[16,16,2]{1,0,2:T(8,128)S(1)} %reshape.91, f32[16,257]{0,1:T(8,128)S(1)} %copy-done.4, ...), kind=kLoop, calls=%fused_computation.20 | loop fusion | flops 723712 | bytes 1372625 | tf_op jit(solution)/shard_map/jit(_where)/select_n | solution.py:65
  85.8 0.4 fusion.13
  86.2 1.8 %copy.83 = f32[16,16,1,256]{3,0,2,1:T(8,128)} copy(f32[16,16,1,256]{1,0,3,2:T(8,128)S(1)} %fusion.13) | data formatting | bytes 524288 | tf_op jit(solution)/shard_map/reshape | solution.py:120
  88.0 3.8 %all-to-all-start = ((f32[16,16,1,256]{3,0,2,1:T(8,128)}), f32[16,16,1,256]{3,0,2,1:T(8,128)S(1)}, u32[]{:S(2)}, u32[]{:S(2)}) async-start(f32[16,16,1,256]{3,0,2,1:T(8,128)} %copy.83), calls=%async_computation | async-start | bytes 524288 | tf_op jit(solution)/shard_map/all_to_all | solution.py:121
  91.9 9.7 %all-to-all-done = f32[16,16,1,256]{3,0,2,1:T(8,128)S(1)} async-done(((f32[16,16,1,256]{3,0,2,1:T(8,128)}), f32[16,16,1,256]{3,0,2,1:T(8,128)S(1)}, u32[]{:S(2)}, u32[]{:S(2)}) %all-to-all-start) | async-done | bytes 262176 | tf_op jit(solution)/shard_map/all_to_all | solution.py:121
  101.5 2.1 %gather_fusion = f32[768,256]{1,0:T(8,128)S(1)} fusion(f32[256,256]{1,0:T(8,128)S(1)} %bitcast.30, s32[1024]{0:T(1024)S(1)} %pad_clamp_fusion.1), kind=kCustom, calls=%fused_computation.clone | custom fusion | bytes 1575936 | tf_op jit(solution)/shard_map/jit(_take)/gather | solution.py:83
  103.6 2.1 %gather_fusion.1 = f32[768,256]{1,0:T(8,128)S(1)} fusion(f32[256,256]{1,0:T(8,128)S(1)} %bitcast.31, s32[1024]{0:T(1024)S(1)} %pad_clamp_fusion), kind=kCustom, calls=%fused_computation.1.clone | custom fusion | bytes 1575936 | tf_op jit(solution)/shard_map/jit(_take)/gather | solution.py:84
  105.8 1.4 %fusion.32 = f32[256,256]{1,0:T(8,128)S(1)} fusion(f32[256,256]{1,0:T(8,128)S(1)} %bitcast.32, f32[768,256]{1,0:T(8,128)S(1)} %gather_fusion.1, f32[768,256]{1,0:T(8,128)S(1)} %gather_fusion, f32[768]{0:T(1024)S(1)} %copy-done.20, s32[768]{0:T(1024)S(1)} %get-tuple-element.13, s32[768]{0:T(1024)S(1)} %get-tuple-element.12, s32[768]{0:T(1024)S(1)} %get-tuple-element.11, ...), kind=kOutput, calls=%fused_computation.79 | convolution fusion | flops 607059968 | bytes 2114048 | tf_op jit(solution)/shard_map/dot_general | solution.py:86
  107.1 2.1 %gather_fusion.2 = f32[768,256]{1,0:T(8,128)S(1)} fusion(f32[256,256]{1,0:T(8,128)S(1)} %fusion.32, s32[1024]{0:T(1024)S(1)} %pad_clamp_fusion.1), kind=kCustom, calls=%fused_computation.2.clone | custom fusion | bytes 1575936 | tf_op jit(solution)/shard_map/jit(_take)/gather | solution.py:83
  109.3 2.1 %gather_fusion.3 = f32[768,256]{1,0:T(8,128)S(1)} fusion(f32[256,256]{1,0:T(8,128)S(1)} %fusion.32, s32[1024]{0:T(1024)S(1)} %pad_clamp_fusion), kind=kCustom, calls=%fused_computation.3.clone | custom fusion | bytes 1575936 | tf_op jit(solution)/shard_map/jit(_take)/gather | solution.py:84
  111.4 1.4 %fusion.31 = f32[256,256]{1,0:T(8,128)S(1)} fusion(f32[256,256]{1,0:T(8,128)S(1)} %fusion.32, f32[768,256]{1,0:T(8,128)S(1)} %gather_fusion.3, f32[768,256]{1,0:T(8,128)S(1)} %gather_fusion.2, f32[768]{0:T(1024)S(1)} %copy-done.20, s32[768]{0:T(1024)S(1)} %get-tuple-element.13, s32[768]{0:T(1024)S(1)} %get-tuple-element.12, s32[768]{0:T(1024)S(1)} %get-tuple-element.11, ...), kind=kOutput, calls=%fused_computation.77 | convolution fusion | flops 607059968 | bytes 2114048 | tf_op jit(solution)/shard_map/dot_general | solution.py:86
  112.7 2.1 %gather_fusion.4 = f32[768,256]{1,0:T(8,128)S(1)} fusion(f32[256,256]{1,0:T(8,128)S(1)} %fusion.31, s32[1024]{0:T(1024)S(1)} %pad_clamp_fusion.1), kind=kCustom, calls=%fused_computation.4.clone | custom fusion | bytes 1575936 | tf_op jit(solution)/shard_map/jit(_take)/gather | solution.py:83
  114.9 2.1 %gather_fusion.5 = f32[768,256]{1,0:T(8,128)S(1)} fusion(f32[256,256]{1,0:T(8,128)S(1)} %fusion.31, s32[1024]{0:T(1024)S(1)} %pad_clamp_fusion), kind=kCustom, calls=%fused_computation.5.clone | custom fusion | bytes 1575936 | tf_op jit(solution)/shard_map/jit(_take)/gather | solution.py:84
  117.0 1.4 %fusion.30 = f32[256,256]{1,0:T(8,128)S(1)} fusion(f32[256,256]{1,0:T(8,128)S(1)} %fusion.31, f32[768,256]{1,0:T(8,128)S(1)} %gather_fusion.5, f32[768,256]{1,0:T(8,128)S(1)} %gather_fusion.4, f32[768]{0:T(1024)S(1)} %copy-done.20, s32[768]{0:T(1024)S(1)} %get-tuple-element.13, s32[768]{0:T(1024)S(1)} %get-tuple-element.12, s32[768]{0:T(1024)S(1)} %get-tuple-element.11, ...), kind=kOutput, calls=%fused_computation.75 | convolution fusion | flops 607059968 | bytes 2114048 | tf_op jit(solution)/shard_map/dot_general | solution.py:86
  118.4 2.1 %gather_fusion.6 = f32[768,256]{1,0:T(8,128)S(1)} fusion(f32[256,256]{1,0:T(8,128)S(1)} %fusion.30, s32[1024]{0:T(1024)S(1)} %pad_clamp_fusion.1), kind=kCustom, calls=%fused_computation.6.clone | custom fusion | bytes 1575936 | tf_op jit(solution)/shard_map/jit(_take)/gather | solution.py:83
  120.5 2.1 %gather_fusion.7 = f32[768,256]{1,0:T(8,128)S(1)} fusion(f32[256,256]{1,0:T(8,128)S(1)} %fusion.30, s32[1024]{0:T(1024)S(1)} %pad_clamp_fusion), kind=kCustom, calls=%fused_computation.7.clone | custom fusion | bytes 1575936 | tf_op jit(solution)/shard_map/jit(_take)/gather | solution.py:84
  122.6 1.4 %fusion.29 = f32[256,256]{1,0:T(8,128)S(1)} fusion(f32[256,256]{1,0:T(8,128)S(1)} %fusion.30, f32[768,256]{1,0:T(8,128)S(1)} %gather_fusion.7, f32[768,256]{1,0:T(8,128)S(1)} %gather_fusion.6, f32[768]{0:T(1024)S(1)} %copy-done.20, s32[768]{0:T(1024)S(1)} %get-tuple-element.13, s32[768]{0:T(1024)S(1)} %get-tuple-element.12, s32[768]{0:T(1024)S(1)} %get-tuple-element.11, ...), kind=kOutput, calls=%fused_computation.73 | convolution fusion | flops 607059968 | bytes 2114048 | tf_op jit(solution)/shard_map/dot_general | solution.py:86
  124.0 2.1 %gather_fusion.8 = f32[768,256]{1,0:T(8,128)S(1)} fusion(f32[256,256]{1,0:T(8,128)S(1)} %fusion.29, s32[1024]{0:T(1024)S(1)} %pad_clamp_fusion.1), kind=kCustom, calls=%fused_computation.8.clone | custom fusion | bytes 1575936 | tf_op jit(solution)/shard_map/jit(_take)/gather | solution.py:83
  126.1 2.4 %gather_fusion.9 = f32[768,256]{1,0:T(8,128)S(1)} fusion(f32[256,256]{1,0:T(8,128)S(1)} %fusion.29, s32[1024]{0:T(1024)S(1)} %pad_clamp_fusion), kind=kCustom, calls=%fused_computation.9.clone | custom fusion | bytes 1575936 | tf_op jit(solution)/shard_map/jit(_take)/gather | solution.py:84
  128.5 1.4 %fusion.28 = f32[256,256]{1,0:T(8,128)S(1)} fusion(f32[256,256]{1,0:T(8,128)S(1)} %fusion.29, f32[768,256]{1,0:T(8,128)S(1)} %gather_fusion.9, f32[768,256]{1,0:T(8,128)S(1)} %gather_fusion.8, f32[768]{0:T(1024)S(1)} %copy-done.20, s32[768]{0:T(1024)S(1)} %get-tuple-element.13, s32[768]{0:T(1024)S(1)} %get-tuple-element.12, s32[768]{0:T(1024)S(1)} %get-tuple-element.11, ...), kind=kOutput, calls=%fused_computation.71 | convolution fusion | flops 607059968 | bytes 2114048 | tf_op jit(solution)/shard_map/dot_general | solution.py:86
  129.8 2.1 %gather_fusion.10 = f32[768,256]{1,0:T(8,128)S(1)} fusion(f32[256,256]{1,0:T(8,128)S(1)} %fusion.28, s32[1024]{0:T(1024)S(1)} %pad_clamp_fusion.1), kind=kCustom, calls=%fused_computation.10.clone | custom fusion | bytes 1575936 | tf_op jit(solution)/shard_map/jit(_take)/gather | solution.py:83
  131.9 2.1 %gather_fusion.11 = f32[768,256]{1,0:T(8,128)S(1)} fusion(f32[256,256]{1,0:T(8,128)S(1)} %fusion.28, s32[1024]{0:T(1024)S(1)} %pad_clamp_fusion), kind=kCustom, calls=%fused_computation.11.clone | custom fusion | bytes 1575936 | tf_op jit(solution)/shard_map/jit(_take)/gather | solution.py:84
  134.1 1.4 %fusion.33 = f32[256,1,256]{2,0,1:T(8,128)S(1)} fusion(f32[256,256]{1,0:T(8,128)S(1)} %fusion.28, f32[768,256]{1,0:T(8,128)S(1)} %gather_fusion.11, f32[768,256]{1,0:T(8,128)S(1)} %gather_fusion.10, f32[768]{0:T(1024)S(1)} %copy-done.20, s32[768]{0:T(1024)S(1)} %get-tuple-element.13, s32[768]{0:T(1024)S(1)} %get-tuple-element.12, ...), kind=kOutput, calls=%fused_computation.80 | convolution fusion | flops 607059968 | bytes 2114048 | tf_op jit(solution)/shard_map/dot_general | solution.py:86
  135.4 1.0 copy.84
  (87 shorter events, 3.2 us)
Async XLA Ops:
  24.9 6.4 %collective-permute-start = (f32[20,4,256]{2,1,0:T(4,128)S(1)}, f32[20,4,256]{2,1,0:T(4,128)S(1)}, u32[]{:S(2)}, u32[]{:S(2)}) collective-permute-start(f32[20,4,256]{2,1,0:T(4,128)S(1)} %get-tuple-element.30), channel_id=1, source_target_pairs={{0,1},{1,0},{2,3},{3,2},{4,5},{5,4},{6,7},{7,6},{8,9},{9,8},{10,11... | collective-permute-start | bytes 245768 | tf_op jit(solution)/shard_map/ppermute | solution.py:22
  26.5 5.0 %collective-permute-start.1 = (f32[20,4,256]{2,1,0:T(4,128)S(1)}, f32[20,4,256]{2,1,0:T(4,128)S(1)}, u32[]{:S(2)}, u32[]{:S(2)}) collective-permute-start(f32[20,4,256]{2,1,0:T(4,128)S(1)} %get-tuple-element.31), channel_id=1, source_target_pairs={{1,0},{0,1},{3,2},{2,3},{5,4},{4,5},{7,6},{6,7},{9,8},{8,9},{11,10... | collective-permute-start | bytes 245768 | tf_op jit(solution)/shard_map/ppermute | solution.py:24
  50.1 2.5 %copy-start.13 = (f32[21,256]{1,0:T(8,128)S(1)}, f32[21,256]{1,0:T(8,128)}, u32[]{:S(2)}) copy-start(f32[21,256]{1,0:T(8,128)} %get-tuple-element.42) | copy-start | bytes 64516
  50.1 6.8 %copy-start.7 = (f32[21,256]{0,1:T(8,128)S(1)}, f32[21,256]{0,1:T(8,128)}, u32[]{:S(2)}) copy-start(f32[21,256]{0,1:T(8,128)} %copy.63) | copy-start | bytes 64516
  56.9 4.8 %copy-start.3 = (f32[16,20,256]{1,0,2:T(8,128)S(1)}, f32[16,20,256]{1,0,2:T(8,128)}, u32[]{:S(2)}) copy-start(f32[16,20,256]{1,0,2:T(8,128)} %copy.86) | copy-start | bytes 983044
  62.3 1.3 copy-start
  63.8 1.7 %copy-start.9 = (f32[20,257]{1,0:T(8,128)S(1)}, f32[20,257]{1,0:T(8,128)}, u32[]{:S(2)}) copy-start(f32[20,257]{1,0:T(8,128)} %get-tuple-element.32) | copy-start | bytes 61684
  63.8 1.8 %copy-start.8 = (f32[20,257]{1,0:T(8,128)S(1)}, f32[20,257]{1,0:T(8,128)}, u32[]{:S(2)}) copy-start(f32[20,257]{1,0:T(8,128)} %get-tuple-element.33) | copy-start | bytes 61684
  63.8 1.9 %copy-start.14 = (pred[20,257]{1,0:T(8,128)(4,1)S(1)}, pred[20,257]{1,0:T(8,128)(4,1)}, u32[]{:S(2)}) copy-start(pred[20,257]{1,0:T(8,128)(4,1)} %get-tuple-element.18) | copy-start | bytes 15424
  63.8 2.1 %copy-start.5 = (f32[20,257]{0,1:T(8,128)S(1)}, f32[20,257]{0,1:T(8,128)}, u32[]{:S(2)}) copy-start(f32[20,257]{0,1:T(8,128)} %copy.71) | copy-start | bytes 61684
  63.8 2.1 %copy-start.19 = (pred[257]{0:T(512)(128)(4,1)S(1)}, pred[257]{0:T(512)(128)(4,1)}, u32[]{:S(2)}) copy-start(pred[257]{0:T(512)(128)(4,1)} %fusion.90) | copy-start | bytes 775
  65.9 6.4 %copy-start.1 = (f32[16,20,256]{1,0,2:T(8,128)S(1)}, f32[16,20,256]{1,0,2:T(8,128)}, u32[]{:S(2)}) copy-start(f32[16,20,256]{1,0,2:T(8,128)} %copy-done) | copy-start | bytes 983044
  73.1 2.0 %copy-start.2 = (f32[16,19,256]{1,0,2:T(8,128)}, f32[16,19,256]{1,0,2:T(8,128)S(1)}, u32[]{:S(2)}) copy-start(f32[16,19,256]{1,0,2:T(8,128)S(1)} %slice_subtract_fusion.4) | copy-start | bytes 933892
  73.2 2.0 %copy-start.12 = (f32[17,256]{1,0:T(8,128)S(1)}, f32[17,256]{1,0:T(8,128)}, u32[]{:S(2)}) copy-start(f32[17,256]{1,0:T(8,128)} %get-tuple-element.40) | copy-start | bytes 52228
  73.2 2.1 %copy-start.11 = (f32[17,256]{1,0:T(8,128)S(1)}, f32[17,256]{1,0:T(8,128)}, u32[]{:S(2)}) copy-start(f32[17,256]{1,0:T(8,128)} %get-tuple-element.41) | copy-start | bytes 52228
  73.2 2.2 %copy-start.15 = (pred[17,256]{1,0:T(8,128)(4,1)S(1)}, pred[17,256]{1,0:T(8,128)(4,1)}, u32[]{:S(2)}) copy-start(pred[17,256]{1,0:T(8,128)(4,1)} %get-tuple-element.16) | copy-start | bytes 13060
  73.2 2.3 %copy-start.6 = (f32[17,256]{0,1:T(8,128)S(1)}, f32[17,256]{0,1:T(8,128)}, u32[]{:S(2)}) copy-start(f32[17,256]{0,1:T(8,128)} %copy.75) | copy-start | bytes 52228
  82.1 0.9 copy-start.4
  82.1 0.9 copy-start.10
  86.2 5.6 %copy-start.17 = (s32[768]{0:T(1024)S(1)}, s32[768]{0:T(1024)}, u32[]{:S(2)}) copy-start(s32[768]{0:T(1024)} %get-tuple-element.45) | copy-start | bytes 9220
  86.2 5.6 %copy-start.16 = (s32[768]{0:T(1024)S(1)}, s32[768]{0:T(1024)}, u32[]{:S(2)}) copy-start(s32[768]{0:T(1024)} %get-tuple-element.44) | copy-start | bytes 9220
  86.2 5.6 %copy-start.18 = (s32[768,2]{0,1:T(2,128)S(1)}, s32[768,2]{0,1:T(2,128)}, u32[]{:S(2)}) copy-start(s32[768,2]{0,1:T(2,128)} %param.11) | copy-start | bytes 18436
  88.0 13.5 %all-to-all-start = ((f32[16,16,1,256]{3,0,2,1:T(8,128)}), f32[16,16,1,256]{3,0,2,1:T(8,128)S(1)}, u32[]{:S(2)}, u32[]{:S(2)}) async-start(f32[16,16,1,256]{3,0,2,1:T(8,128)} %copy.83), calls=%async_computation | async-start | bytes 524288 | tf_op jit(solution)/shard_map/all_to_all | solution.py:121
  103.6 2.1 %copy-start.20 = (f32[768]{0:T(1024)S(1)}, f32[768]{0:T(1024)}, u32[]{:S(2)}) copy-start(f32[768]{0:T(1024)} %param.9) | copy-start | bytes 9220
where the time goes:
time: 137 us; the launch traced here: 136 us
  local copies, waits for them, and re-layouts  52.4 us (38%)
  other arithmetic  36.3 us (26%)
  blocking collectives  23.2 us (17%)
  waiting for transfers between devices  9.79 us (7%)
  matrix products  8.2 us (6%)
  starting transfers between devices  5.84 us (4%)
    all_gather x1, blocking collectives, on_device(): lax.all_gather(planes, 'wide', axis=1, tiled=True).astype(jnp.float32)  23.2 us
    unnamed x49, local copies, waits for them, and re-layouts  15.1 us
    gather x6, local copies, waits for them, and re-layouts, react_cells(): jnp.take(cell_block, second_ids, axis=0)  12.9 us
    gather x6, local copies, waits for them, and re-layouts, react_cells(): jnp.take(cell_block, first_ids, axis=0)  12.6 us
    sub x2, other arithmetic, sweep_axis(): inner_speed * jnp.where(inner_speed >= 0.0, left_value, right_value)  9.84 us
    all_to_all x1, waiting for transfers between devices, on_device(): lax.all_to_all(shaped, 'wide', split_axis=1, concat_axis=0, tiled=True)  9.66 us
    select_n x2, other arithmetic, sweep_axis(): jnp.where((position > 0) & (position < length - 4), face_flux, 0.0)  9.12 us
    dot_general x6, matrix products, react_cells(): jnp.dot(net_matrix, rate_values, precision=lax.Precision.HIGHEST)  8.2 us
  transfers between devices with their start and end apart: 3, of which 2 were waited for; matrix products, arithmetic and copies ran while one was open for 3% of the time, Pallas kernels for 0%

commit v1 on v0

v1 whole, which is shorter than its diff:
```python
import functools
import jax
import jax.numpy as jnp
from jax import lax
from jax.experimental import pallas as pl
from jax.experimental.pallas import tpu as pltpu
from jax.sharding import PartitionSpec as P

SECTIONS = 6
DIFFUSION = 0.1
CHEM_STEP = 0.02
HALO = 4
CHUNK = 4
MESH = pl.DeviceIdType.MESH
F32 = jnp.float32
BF16 = jnp.bfloat16


def minmod(first, second):
    return jnp.maximum(0.0, jnp.minimum(first, second)) + jnp.minimum(
        0.0, jnp.maximum(first, second)
    )


def coefficients(a):
    size = jnp.abs(a)
    return jnp.minimum(a, 0.0) - DIFFUSION, 0.5 * size * (1.0 - size), a >= 0.0


def sweep_rows(ext, wind):
    m = ext.shape[0] - 4
    a = 0.5 * (wind[1 : m + 2] + wind[2 : m + 3])
    jump_gain, slope_gain, forward = coefficients(a)
    jumps = ext[1:] - ext[:-1]
    slopes = minmod(jumps[:-1], jumps[1:])
    flux = (
        a * ext[1 : m + 2]
        + jump_gain * jumps[1 : m + 2]
        + slope_gain * jnp.where(forward, slopes[: m + 1], slopes[1:])
    )
    return ext[2 : m + 2] - (flux[1:] - flux[:-1])


def sweep_columns(q, wind):
    columns = q.shape[2]
    last = lax.broadcasted_iota(jnp.int32, wind.shape, 2) == columns - 1
    a = jnp.where(last, 0.0, 0.5 * (wind + pltpu.roll(wind, columns - 1, 2)))
    jump_gain, slope_gain, forward = coefficients(a)
    edge = lax.broadcasted_iota(jnp.int32, q.shape, 2) == columns - 1
    jumps = jnp.where(edge, 0.0, pltpu.roll(q, columns - 1, 2) - q)
    slopes = minmod(pltpu.roll(jumps, 1, 2), jumps)
    upwind = jnp.where(forward, slopes, pltpu.roll(slopes, columns - 1, 2))
    flux = a * q + jump_gain * jumps + slope_gain * upwind
    return q - (flux - pltpu.roll(flux, 1, 2))


def kernel(
    conc_ref, wind_ref, k_ref, react_ref, prod_ref, out_ref,
    ext, mid, done, winds, windf, incoming, cells, split, picks, net, gain, rates,
    wind_send, wind_recv, rim_send, rim_recv, halo_send, halo_recv, row_send, row_recv,
):
    wide = lax.axis_size("wide")
    narrow = lax.axis_size("narrow")
    me = lax.axis_index("wide")
    slab = lax.axis_index("narrow")
    groups, rows, columns = conc_ref.shape
    species = cells.shape[0]
    reactions = k_ref.shape[1]
    above = lax.rem(slab + 1, narrow)
    below = lax.rem(slab + narrow - 1, narrow)

    barrier = pltpu.get_barrier_semaphore()
    for step in range(1, wide):
        pl.semaphore_signal(
            barrier, inc=1, device_id={"wide": lax.rem(me + step, wide)}, device_id_type=MESH
        )
    for other in (above, below):
        pl.semaphore_signal(barrier, inc=1, device_id={"narrow": other}, device_id_type=MESH)

    ext[HALO : HALO + rows] = jnp.swapaxes(conc_ref[...], 0, 1)
    winds[HALO + me] = wind_ref[...]

    pl.semaphore_wait(barrier, wide + 1)

    def wind_copy(step):
        there = lax.rem(me + step, wide)
        return pltpu.make_async_remote_copy(
            src_ref=wind_ref,
            dst_ref=winds.at[HALO + me],
            send_sem=wind_send.at[step],
            recv_sem=wind_recv.at[me],
            device_id={"wide": there},
            device_id_type=MESH,
        )

    def halo_copies(buffer, send, recv):
        up = pltpu.make_async_remote_copy(
            src_ref=buffer.at[pl.ds(rows, HALO)],
            dst_ref=buffer.at[pl.ds(0, HALO)],
            send_sem=send.at[0],
            recv_sem=recv.at[0],
            device_id={"narrow": above},
            device_id_type=MESH,
        )
        down = pltpu.make_async_remote_copy(
            src_ref=buffer.at[pl.ds(HALO, HALO)],
            dst_ref=buffer.at[pl.ds(HALO + rows, HALO)],
            send_sem=send.at[1],
            recv_sem=recv.at[1],
            device_id={"narrow": below},
            device_id_type=MESH,
        )
        return up, down

    wind_copies = [wind_copy(step) for step in range(1, wide)]
    for copy in wind_copies:
        copy.start()
    halos = halo_copies(ext, halo_send, halo_recv)
    for copy in halos:
        copy.start()

    ids = lax.broadcasted_iota(jnp.int32, (species, reactions), 0)

    def one_hot(ref, which):
        return jnp.where(ids == ref[which : which + 1, :], 1.0, 0.0)

    first, second = one_hot(react_ref, 0), one_hot(react_ref, 1)
    net[...] = (one_hot(prod_ref, 0) + one_hot(prod_ref, 1) - first - second).astype(BF16)
    for index, table in enumerate((first, second)):
        turned = jnp.transpose(table).astype(BF16)
        picks[index, :, :species] = turned
        picks[index, :, species:] = turned
    gain[...] = jnp.transpose(jnp.broadcast_to(CHEM_STEP * k_ref[...], (columns, reactions)))

    for step in range(1, wide):
        source = lax.rem(me + wide - step, wide)
        pltpu.make_async_remote_copy(
            src_ref=wind_ref,
            dst_ref=winds.at[HALO + source],
            send_sem=wind_send.at[step],
            recv_sem=wind_recv.at[source],
            device_id={"wide": source},
            device_id_type=MESH,
        ).wait_recv()
    rims = halo_copies(winds, rim_send, rim_recv)
    for copy in rims:
        copy.start()
    windf[HALO : HALO + rows] = winds[HALO : HALO + rows].astype(F32)

    def wind_of(substep, direction, start, count):
        return windf[start : start + count, substep, direction : direction + 1, :]

    def first_substep(o):
        swept = sweep_rows(ext[o : o + CHUNK + 4], wind_of(0, 0, o, CHUNK + 4))
        mid[o : o + CHUNK] = sweep_columns(swept, wind_of(0, 1, o + 2, CHUNK))

    def second_substep(g):
        swept = sweep_rows(mid[g : g + CHUNK + 4], wind_of(1, 0, g + 2, CHUNK + 4))
        done[g : g + CHUNK] = sweep_columns(swept, wind_of(1, 1, g + 4, CHUNK))

    def row_copy(row):
        return pltpu.make_async_remote_copy(
            src_ref=done.at[row],
            dst_ref=incoming.at[me],
            send_sem=row_send.at[row],
            recv_sem=row_recv.at[me],
            device_id={"wide": row},
            device_id_type=MESH,
        )

    def send_row(row):
        @pl.when(row != me)
        def _():
            row_copy(row).start()

    inner = rows - 2 * HALO
    for o in range(HALO, rows, CHUNK):
        first_substep(o)
    for g in range(HALO, rows - HALO, CHUNK):
        second_substep(g)
    for k in range(inner):
        send_row(HALO + lax.rem(me + k, inner))

    for copy in halos + rims:
        copy.wait_recv()
    windf[0:HALO] = winds[0:HALO].astype(F32)
    windf[HALO + rows :] = winds[HALO + rows :].astype(F32)
    for o in (0, rows):
        first_substep(o)
    for g in (0, rows - HALO):
        second_substep(g)
    for k in range(2 * HALO):
        index = lax.rem(me + k, 2 * HALO)
        send_row(index + inner * (index // HALO))

    incoming[me] = done[me]
    for source in range(wide):
        @pl.when(source != me)
        def _():
            pltpu.make_async_remote_copy(
                src_ref=done.at[source],
                dst_ref=incoming.at[source],
                send_sem=row_send.at[source],
                recv_sem=row_recv.at[source],
                device_id={"wide": source},
                device_id_type=MESH,
            ).wait_recv()

    for source in range(wide):
        cells[source * groups : (source + 1) * groups] = incoming[source]

    block = species

    def section(_, carry):
        q = cells[...]
        high = q.astype(BF16)
        split[:species] = high
        split[species:] = (q - high.astype(F32)).astype(BF16)
        for start in range(0, reactions, block):
            span = pl.ds(start, block)
            one = jnp.dot(picks[0, span, :], split[...], preferred_element_type=F32)
            two = jnp.dot(picks[1, span, :], split[...], preferred_element_type=F32)
            rates[span, :] = (gain[span, :] * one * two).astype(BF16)
        cells[...] = q + jnp.dot(net[...], rates[...], preferred_element_type=F32)
        return carry

    lax.fori_loop(0, SECTIONS, section, 0)
    out_ref[...] = cells[...]

    for copy in wind_copies:
        copy.wait_send()
    for copy in halos + rims:
        copy.wait_send()
    for row in range(rows):
        @pl.when(row != me)
        def _():
            row_copy(row).wait_send()


def on_device(wide, concentrations, wind_speeds, rate_constants, reactants, products):
    groups, rows, columns = concentrations.shape
    assert wind_speeds.shape[2] == 1 and rows == wide and rows % CHUNK == 0
    species = groups * wide
    reactions = rate_constants.shape[0]
    wind = jnp.swapaxes(wind_speeds, 1, 2).reshape(2, 2, columns)
    dma = pltpu.SemaphoreType.DMA
    result = pl.pallas_call(
        kernel,
        out_shape=jax.ShapeDtypeStruct((species, columns), F32),
        in_specs=[pl.BlockSpec(memory_space=pltpu.VMEM)] * 5,
        out_specs=pl.BlockSpec(memory_space=pltpu.VMEM),
        scratch_shapes=[
            pltpu.VMEM((rows + 2 * HALO, groups, columns), F32),
            pltpu.VMEM((rows + HALO, groups, columns), F32),
            pltpu.VMEM((rows, groups, columns), F32),
            pltpu.VMEM((rows + 2 * HALO, 2, 2, columns), BF16),
            pltpu.VMEM((rows + 2 * HALO, 2, 2, columns), F32),
            pltpu.VMEM((wide, groups, columns), F32),
            pltpu.VMEM((species, columns), F32),
            pltpu.VMEM((2 * species, columns), BF16),
            pltpu.VMEM((2, reactions, 2 * species), BF16),
            pltpu.VMEM((species, reactions), BF16),
            pltpu.VMEM((reactions, columns), F32),
            pltpu.VMEM((reactions, columns), BF16),
            dma((wide,)), dma((wide,)), dma((2,)), dma((2,)),
            dma((2,)), dma((2,)), dma((rows,)), dma((wide,)),
        ],
        compiler_params=pltpu.CompilerParams(collective_id=0, has_side_effects=True),
        name="transport_chemistry",
    )(concentrations, wind, rate_constants.reshape(1, reactions), reactants.T, products.T)
    return result.reshape(species, 1, columns)


def solution(mesh):
    return jax.shard_map(
        functools.partial(on_device, mesh.shape["wide"]),
        mesh=mesh,
        in_specs=(
            P("wide", "narrow", None),
            P(None, None, ("narrow", "wide"), None),
            P(),
            P(),
            P(),
        ),
        out_specs=P(None, ("narrow", "wide"), None),
        check_vma=False,
    )
```

time: 137 us -> 30.3 us (0.22)
  local copies, waits for them, and re-layouts: 52.4 us -> 3.19 us
  other arithmetic: 36.3 us -> 0 us
  Pallas kernels: 0 us -> 26.9 us
  blocking collectives: 23.2 us -> 0 us
  waiting for transfers between devices: 9.79 us -> 0 us
  matrix products: 8.2 us -> 0 us
  starting transfers between devices: 5.84 us -> 0 us
    pallas_call x0 -> x1, Pallas kernels: none -> 26.9 us  [on_device(): pl.pallas_call(kernel, out_shape=jax.ShapeDtypeStruct((species, columns),...]
    gather x12 -> x0, local copies, waits for them, and re-layouts: 25.6 us -> none  [the longest x6 12.9 us: react_cells(): jnp.take(cell_block, second_ids, axis=0)]
    all_gather x1 -> x0, blocking collectives: 23.2 us -> none  [on_device(): lax.all_gather(planes, 'wide', axis=1, tiled=True).astype(jnp.float32)]
    sub x9 -> x0, other arithmetic: 15.2 us -> none  [the longest x2 9.84 us: sweep_axis(): inner_speed * jnp.where(inner_speed >= 0.0, left_value, right_value)]
    unnamed x49 -> x2, local copies, waits for them, and re-layouts: 15.1 us -> 0.69 us
    select_n x3 -> x0, other arithmetic: 9.72 us -> none  [the longest x2 9.12 us: sweep_axis(): jnp.where((position > 0) & (position < length - 4), face_flux, 0.0)]
    all_to_all x1 -> x0, waiting for transfers between devices: 9.66 us -> none  [on_device(): lax.all_to_all(shaped, 'wide', split_axis=1, concat_axis=0, tiled=True)]
    dot_general x6 -> x0, matrix products: 8.2 us -> none  [react_cells(): jnp.dot(net_matrix, rate_values, precision=lax.Precision.HIGHEST)]
  transfers between devices with their start and end apart: 3 -> 0, of which waited for: 2 -> 0; matrix products, arithmetic and copies ran while one was open for 3% -> 0% of each run, Pallas kernels for 0% -> 0%
where the time goes in v1:
time: 30.3 us; the launch traced here: 30.1 us
  Pallas kernels  26.9 us (89%)
  local copies, waits for them, and re-layouts  3.19 us (11%)
    pallas_call x1, Pallas kernels, on_device(): pl.pallas_call(kernel, out_shape=jax.ShapeDtypeStruct((species, columns),...  26.9 us
    reshape x1, local copies, waits for them, and re-layouts, on_device(): return result.reshape(species, 1, columns)  1.92 us
    unnamed x2, local copies, waits for them, and re-layouts  0.69 us

profile of v1, /device:TPU:0, one launch (start us, length us, event | category | flops | bytes accessed | tf_op | source)
XLA Modules:
  0.0 30.1 jit_solution(10962925461955679782)
XLA Ops:
  0.0 0.0 copy-start
  0.0 0.7 %copy-done = f32[768]{0:T(1024)S(1)} copy-done((f32[768]{0:T(1024)S(1)}, f32[768]{0:T(1024)}, u32[]{:S(2)}) %copy-start) | copy-done | bytes 3096
  0.7 0.6 %reshape.6.k_ref = f32[1,768]{1,0:T(1,128)} reshape(f32[768]{0:T(1024)S(1)} %copy-done) | data formatting | bytes 6144 | tf_op jit(solution)/shard_map/reshape | solution.py:270
  1.3 26.9 %transport_chemistry.1 = f32[256,256]{1,0:T(8,128)} custom-call(f32[16,16,256]{2,1,0:T(8,128)} %conc_ref.1, bf16[2,2,256]{2,1,0:T(2,128)(2,1)} %bitcast.7, f32[1,768]{1,0:T(1,128)} %reshape.6.k_ref, s32[2,768]{1,0:T(2,128)} %bitcast.5, s32[2,768]{1,0:T(2,128)} %bitcast.6), custom_call_target="tpu_custom_call" | custom-call | tf_op jit(solution)/shard_map/transport_chemistry/pallas_call | solution.py:247
  28.2 1.9 %copy.6 = f32[256,1,256]{2,1,0:T(1,128)} copy(f32[256,1,256]{2,0,1:T(8,128)} %bitcast.4) | data formatting | bytes 524288 | tf_op jit(solution)/shard_map/reshape | solution.py:271
Async XLA Ops:
  0.0 0.7 %copy-start = (f32[768]{0:T(1024)S(1)}, f32[768]{0:T(1024)}, u32[]{:S(2)}) copy-start(f32[768]{0:T(1024)} %param.7) | copy-start | bytes 9220

commit v2 on v1

--- a/solution.py
+++ b/solution.py
@@ -55,9 +55,10 @@
 
 
 def kernel(
-    conc_ref, wind_ref, k_ref, react_ref, prod_ref, out_ref,
-    ext, mid, done, winds, windf, incoming, cells, split, picks, net, gain, rates,
-    wind_send, wind_recv, rim_send, rim_recv, halo_send, halo_recv, row_send, row_recv,
+    conc_in, wind_ref, k_in, react_in, prod_in, out_ref,
+    conc_ref, k_ref, react_ref, prod_ref,
+    ext, mid, done, winds, windf, incoming, cells, cells_left, picks, net, gain, rates, rates_left,
+    wind_send, wind_recv, rim_send, halo_send, halo_recv, row_send, row_recv, load_sem,
 ):
     wide = lax.axis_size("wide")
     narrow = lax.axis_size("narrow")
@@ -65,7 +66,8 @@
     slab = lax.axis_index("narrow")
     groups, rows, columns = conc_ref.shape
     species = cells.shape[0]
-    reactions = k_ref.shape[1]
+    reactions = react_ref.shape[1]
+    lanes = k_ref.shape[1]
     above = lax.rem(slab + 1, narrow)
     below = lax.rem(slab + narrow - 1, narrow)
 
@@ -77,21 +79,75 @@
     for other in (above, below):
         pl.semaphore_signal(barrier, inc=1, device_id={"narrow": other}, device_id_type=MESH)
 
-    ext[HALO : HALO + rows] = jnp.swapaxes(conc_ref[...], 0, 1)
-    winds[HALO + me] = wind_ref[...]
-
-    pl.semaphore_wait(barrier, wide + 1)
-
-    def wind_copy(step):
-        there = lax.rem(me + step, wide)
+    for place in range(HALO):
+        pl.semaphore_signal(
+            barrier, inc=1, device_id={"narrow": above, "wide": place}, device_id_type=MESH
+        )
+        pl.semaphore_signal(
+            barrier,
+            inc=1,
+            device_id={"narrow": below, "wide": wide - 1 - place},
+            device_id_type=MESH,
+        )
+
+    loads = [
+        pltpu.make_async_copy(source, target, load_sem.at[index])
+        for index, (source, target) in enumerate(
+            (
+                (conc_in, conc_ref),
+                (react_in, react_ref),
+                (prod_in, prod_ref),
+                (k_in, k_ref),
+                (wind_ref, winds.at[HALO + me]),
+            )
+        )
+    ]
+    for copy in loads:
+        copy.start()
+
+    low_rim = (wide - 1 - me + HALO) // wide
+    high_rim = (me + HALO) // wide
+    pl.semaphore_wait(barrier, wide + 1 + wide * (low_rim + high_rim))
+
+    def wind_copy(slot, send, **device):
         return pltpu.make_async_remote_copy(
             src_ref=wind_ref,
-            dst_ref=winds.at[HALO + me],
-            send_sem=wind_send.at[step],
-            recv_sem=wind_recv.at[me],
-            device_id={"wide": there},
-            device_id_type=MESH,
-        )
+            dst_ref=winds.at[slot],
+            send_sem=send,
+            recv_sem=wind_recv.at[slot],
+            device_id=device,
+            device_id_type=MESH,
+        )
+
+    wind_copies = [
+        wind_copy(HALO + me, wind_send.at[step], wide=lax.rem(me + step, wide))
+        for step in range(1, wide)
+    ]
+
+    def rim_copies(act):
+        @pl.when(me < HALO)
+        def _():
+            for step in range(wide):
+                act(
+                    wind_copy(
+                        HALO + rows + me,
+                        rim_send.at[0, step],
+                        narrow=below,
+                        wide=lax.rem(me + step, wide),
+                    )
+                )
+
+        @pl.when(me >= wide - HALO)
+        def _():
+            for step in range(wide):
+                act(
+                    wind_copy(
+                        me - (wide - HALO),
+                        rim_send.at[1, step],
+                        narrow=above,
+                        wide=lax.rem(me + step, wide),
+                    )
+                )
 
     def halo_copies(buffer, send, recv):
         up = pltpu.make_async_remote_copy(
@@ -112,13 +168,18 @@
         )
         return up, down
 
-    wind_copies = [wind_copy(step) for step in range(1, wide)]
     for copy in wind_copies:
         copy.start()
+    rim_copies(lambda copy: copy.start())
+
+    loads[0].wait()
+    ext[HALO : HALO + rows] = jnp.swapaxes(conc_ref[...], 0, 1)
     halos = halo_copies(ext, halo_send, halo_recv)
     for copy in halos:
         copy.start()
 
+    for copy in loads[1:]:
+        copy.wait()
     ids = lax.broadcasted_iota(jnp.int32, (species, reactions), 0)
 
     def one_hot(ref, which):
@@ -127,24 +188,23 @@
     first, second = one_hot(react_ref, 0), one_hot(react_ref, 1)
     net[...] = (one_hot(prod_ref, 0) + one_hot(prod_ref, 1) - first - second).astype(BF16)
     for index, table in enumerate((first, second)):
-        turned = jnp.transpose(table).astype(BF16)
-        picks[index, :, :species] = turned
-        picks[index, :, species:] = turned
-    gain[...] = jnp.transpose(jnp.broadcast_to(CHEM_STEP * k_ref[...], (columns, reactions)))
-
-    for step in range(1, wide):
-        source = lax.rem(me + wide - step, wide)
-        pltpu.make_async_remote_copy(
-            src_ref=wind_ref,
-            dst_ref=winds.at[HALO + source],
-            send_sem=wind_send.at[step],
-            recv_sem=wind_recv.at[source],
-            device_id={"wide": source},
-            device_id_type=MESH,
-        ).wait_recv()
-    rims = halo_copies(winds, rim_send, rim_recv)
-    for copy in rims:
-        copy.start()
+        picks[index] = jnp.transpose(table).astype(BF16)
+    for part in range(reactions // lanes):
+        constants = CHEM_STEP * k_ref[part : part + 1, :]
+        gain[part * lanes : (part + 1) * lanes] = jnp.transpose(
+            jnp.broadcast_to(constants, (columns, lanes))
+        )
+    cells_left[...] = jnp.zeros_like(cells_left)
+    rates_left[...] = jnp.zeros_like(rates_left)
+
+    def wind_arrival(slot):
+        wind_copy(slot, wind_send.at[0], wide=lax.rem(me + 1, wide)).wait_recv()
+
+    for source in range(wide):
+        @pl.when(source != me)
+        def _():
+            wind_arrival(HALO + source)
+
     windf[HALO : HALO + rows] = winds[HALO : HALO + rows].astype(F32)
 
     def wind_of(substep, direction, start, count):
@@ -181,7 +241,10 @@
     for k in range(inner):
         send_row(HALO + lax.rem(me + k, inner))
 
-    for copy in halos + rims:
+    for slot in range(HALO):
+        wind_arrival(slot)
+        wind_arrival(HALO + rows + slot)
+    for copy in halos:
         copy.wait_recv()
     windf[0:HALO] = winds[0:HALO].astype(F32)
     windf[HALO + rows :] = winds[HALO + rows :].astype(F32)
@@ -213,23 +276,29 @@
 
     def section(_, carry):
         q = cells[...]
-        high = q.astype(BF16)
-        split[:species] = high
-        split[species:] = (q - high.astype(F32)).astype(BF16)
+        wanted = q + cells_left[...]
+        high = wanted.astype(BF16)
+        cells_left[...] = wanted - high.astype(F32)
         for start in range(0, reactions, block):
             span = pl.ds(start, block)
-            one = jnp.dot(picks[0, span, :], split[...], preferred_element_type=F32)
-            two = jnp.dot(picks[1, span, :], split[...], preferred_element_type=F32)
-            rates[span, :] = (gain[span, :] * one * two).astype(BF16)
+            one = jnp.dot(picks[0, span, :], high, preferred_element_type=F32)
+            two = jnp.dot(picks[1, span, :], high, preferred_element_type=F32)
+            rate = gain[span, :] * one * two + rates_left[span, :]
+            rounded = rate.astype(BF16)
+            rates_left[span, :] = rate - rounded.astype(F32)
+            rates[span, :] = rounded
         cells[...] = q + jnp.dot(net[...], rates[...], preferred_element_type=F32)
         return carry
 
     lax.fori_loop(0, SECTIONS, section, 0)
-    out_ref[...] = cells[...]
+    parts = columns // lanes
+    for part in range(parts):
+        out_ref[pl.ds(part, species, stride=parts), :] = cells[:, part * lanes : (part + 1) * lanes]
 
     for copy in wind_copies:
         copy.wait_send()
-    for copy in halos + rims:
+    rim_copies(lambda copy: copy.wait_send())
+    for copy in halos:
         copy.wait_send()
     for row in range(rows):
         @pl.when(row != me)
@@ -239,17 +308,22 @@
 
 def on_device(wide, concentrations, wind_speeds, rate_constants, reactants, products):
     groups, rows, columns = concentrations.shape
-    assert wind_speeds.shape[2] == 1 and rows == wide and rows % CHUNK == 0
+    assert wind_speeds.shape[2] == 1 and 2 * HALO <= rows and rows == wide and rows % CHUNK == 0
     species = groups * wide
     reactions = rate_constants.shape[0]
     wind = jnp.swapaxes(wind_speeds, 1, 2).reshape(2, 2, columns)
+    lanes = 128
     dma = pltpu.SemaphoreType.DMA
     result = pl.pallas_call(
         kernel,
-        out_shape=jax.ShapeDtypeStruct((species, columns), F32),
-        in_specs=[pl.BlockSpec(memory_space=pltpu.VMEM)] * 5,
+        out_shape=jax.ShapeDtypeStruct((species * columns // lanes, lanes), F32),
+        in_specs=[pl.BlockSpec(memory_space=pl.ANY)] * 5,
         out_specs=pl.BlockSpec(memory_space=pltpu.VMEM),
         scratch_shapes=[
+            pltpu.VMEM((groups, rows, columns), F32),
+            pltpu.VMEM((reactions // lanes, lanes), F32),
+            pltpu.VMEM((2, reactions), jnp.int32),
+            pltpu.VMEM((2, reactions), jnp.int32),
             pltpu.VMEM((rows + 2 * HALO, groups, columns), F32),
             pltpu.VMEM((rows + HALO, groups, columns), F32),
             pltpu.VMEM((rows, groups, columns), F32),
@@ -257,17 +331,18 @@
             pltpu.VMEM((rows + 2 * HALO, 2, 2, columns), F32),
             pltpu.VMEM((wide, groups, columns), F32),
             pltpu.VMEM((species, columns), F32),
-            pltpu.VMEM((2 * species, columns), BF16),
-            pltpu.VMEM((2, reactions, 2 * species), BF16),
+            pltpu.VMEM((species, columns), F32),
+            pltpu.VMEM((2, reactions, species), BF16),
             pltpu.VMEM((species, reactions), BF16),
             pltpu.VMEM((reactions, columns), F32),
             pltpu.VMEM((reactions, columns), BF16),
-            dma((wide,)), dma((wide,)), dma((2,)), dma((2,)),
-            dma((2,)), dma((2,)), dma((rows,)), dma((wide,)),
+            pltpu.VMEM((reactions, columns), F32),
+            dma((wide,)), dma((rows + 2 * HALO,)), dma((2, wide)),
+            dma((2,)), dma((2,)), dma((rows,)), dma((wide,)), dma((5,)),
         ],
         compiler_params=pltpu.CompilerParams(collective_id=0, has_side_effects=True),
         name="transport_chemistry",
-    )(concentrations, wind, rate_constants.reshape(1, reactions), reactants.T, products.T)
+    )(concentrations, wind, rate_constants.reshape(-1, lanes), reactants.T, products.T)
     return result.reshape(species, 1, columns)
 
 

time: 30.3 us -> 28.1 us (0.927)
  local copies, waits for them, and re-layouts: 3.19 us -> 1.83 us
  Pallas kernels: 26.9 us -> 26.1 us
    reshape x2 -> x0, local copies, waits for them, and re-layouts: 2.5 us -> none  [the longest x1 1.92 us: on_device(): return result.reshape(species, 1, columns)]
    unnamed x2 -> x1, local copies, waits for them, and re-layouts: 0.69 us -> 1.83 us
    pallas_call x1, Pallas kernels: 26.9 us -> 26.1 us  [on_device(): pl.pallas_call(kernel, out_shape=jax.ShapeDtypeStruct((species * columns...]
where the time goes in v2:
time: 28.1 us; the launch traced here: 27.9 us
  Pallas kernels  26.1 us (93%)
  local copies, waits for them, and re-layouts  1.83 us (7%)
    pallas_call x1, Pallas kernels, on_device(): pl.pallas_call(kernel, out_shape=jax.ShapeDtypeStruct((species * columns...  26.1 us
    unnamed x1, local copies, waits for them, and re-layouts  1.83 us

profile of v2, /device:TPU:0, one launch (start us, length us, event | category | flops | bytes accessed | tf_op | source)
XLA Modules:
  0.0 27.9 jit_solution(14832617087826818250)
XLA Ops:
  0.0 26.1 %transport_chemistry.1 = f32[512,128]{1,0:T(8,128)} custom-call(f32[16,16,256]{2,1,0:T(8,128)} %conc_in.1, bf16[2,2,256]{2,1,0:T(2,128)(2,1)} %bitcast.9, f32[6,128]{1,0:T(8,128)} %bitcast.8, s32[2,768]{1,0:T(2,128)} %bitcast.6, s32[2,768]{1,0:T(2,128)} %bitcast.7), custom_call_target="tpu_custom_call" | custom-call | tf_op jit(solution)/shard_map/transport_chemistry/pallas_call | solution.py:317
  26.1 1.8 %copy.8 = f32[256,1,256]{2,1,0:T(1,128)} copy(f32[256,1,256]{2,1,0:T(1,128)} %bitcast.5) | data formatting | bytes 524288

commit v3 on v2

--- a/solution.py
+++ b/solution.py
@@ -14,6 +14,19 @@
 MESH = pl.DeviceIdType.MESH
 F32 = jnp.float32
 BF16 = jnp.bfloat16
+
+
+MIDDLE = 1.05
+REACH = 0.95
+TOP_CODE = 32760.0
+
+
+def to_codes(scaled):
+    return jnp.round(scaled).astype(jnp.int32).astype(jnp.int16)
+
+
+def from_codes(codes):
+    return codes.astype(jnp.int32).astype(F32)
 
 
 def minmod(first, second):
@@ -57,7 +70,7 @@
 def kernel(
     conc_in, wind_ref, k_in, react_in, prod_in, out_ref,
     conc_ref, k_ref, react_ref, prod_ref,
-    ext, mid, done, winds, windf, incoming, cells, cells_left, picks, net, gain, rates, rates_left,
+    ext, mid, rims_out, rims_in, codes, tops, winds, windf, codes_in, tops_in, cells, cells_left, picks, net, gain, rates, rates_left,
     wind_send, wind_recv, rim_send, halo_send, halo_recv, row_send, row_recv, load_sem,
 ):
     wide = lax.axis_size("wide")
@@ -149,32 +162,27 @@
                     )
                 )
 
-    def halo_copies(buffer, send, recv):
-        up = pltpu.make_async_remote_copy(
-            src_ref=buffer.at[pl.ds(rows, HALO)],
-            dst_ref=buffer.at[pl.ds(0, HALO)],
-            send_sem=send.at[0],
-            recv_sem=recv.at[0],
-            device_id={"narrow": above},
+    halos = [
+        pltpu.make_async_remote_copy(
+            src_ref=rims_out.at[side],
+            dst_ref=rims_in.at[side],
+            send_sem=halo_send.at[side],
+            recv_sem=halo_recv.at[side],
+            device_id={"narrow": other},
             device_id_type=MESH,
         )
-        down = pltpu.make_async_remote_copy(
-            src_ref=buffer.at[pl.ds(HALO, HALO)],
-            dst_ref=buffer.at[pl.ds(HALO + rows, HALO)],
-            send_sem=send.at[1],
-            recv_sem=recv.at[1],
-            device_id={"narrow": below},
-            device_id_type=MESH,
-        )
-        return up, down
+        for side, other in enumerate((above, below))
+    ]
 
     for copy in wind_copies:
         copy.start()
     rim_copies(lambda copy: copy.start())
 
     loads[0].wait()
-    ext[HALO : HALO + rows] = jnp.swapaxes(conc_ref[...], 0, 1)
-    halos = halo_copies(ext, halo_send, halo_recv)
+    turned = jnp.swapaxes(conc_ref[...], 0, 1)
+    ext[HALO : HALO + rows] = turned
+    for side, rim in enumerate((turned[rows - HALO :], turned[:HALO])):
+        rims_out[side] = to_codes((rim - MIDDLE) * (TOP_CODE / REACH))
     for copy in halos:
         copy.start()
 
@@ -216,22 +224,29 @@
 
     def second_substep(g):
         swept = sweep_rows(mid[g : g + CHUNK + 4], wind_of(1, 0, g + 2, CHUNK + 4))
-        done[g : g + CHUNK] = sweep_columns(swept, wind_of(1, 1, g + 4, CHUNK))
-
-    def row_copy(row):
-        return pltpu.make_async_remote_copy(
-            src_ref=done.at[row],
-            dst_ref=incoming.at[me],
-            send_sem=row_send.at[row],
-            recv_sem=row_recv.at[me],
-            device_id={"wide": row},
-            device_id_type=MESH,
-        )
+        value = sweep_columns(swept, wind_of(1, 1, g + 4, CHUNK))
+        top = jnp.maximum(jnp.max(jnp.abs(value), axis=1, keepdims=True), 1e-30)
+        codes[g : g + CHUNK] = to_codes(value * (TOP_CODE / top))
+        tops[g : g + CHUNK] = top * (1.0 / TOP_CODE)
+
+    def row_copies(row, source):
+        return [
+            pltpu.make_async_remote_copy(
+                src_ref=here.at[row],
+                dst_ref=there.at[source],
+                send_sem=row_send.at[index, row],
+                recv_sem=row_recv.at[index, source],
+                device_id={"wide": row},
+                device_id_type=MESH,
+            )
+            for index, (here, there) in enumerate(((codes, codes_in), (tops, tops_in)))
+        ]
 
     def send_row(row):
         @pl.when(row != me)
         def _():
-            row_copy(row).start()
+            for copy in row_copies(row, me):
+                copy.start()
 
     inner = rows - 2 * HALO
     for o in range(HALO, rows, CHUNK):
@@ -246,6 +261,8 @@
         wind_arrival(HALO + rows + slot)
     for copy in halos:
         copy.wait_recv()
+    for side, start in enumerate((0, HALO + rows)):
+        ext[start : start + HALO] = from_codes(rims_in[side]) * (REACH / TOP_CODE) + MIDDLE
     windf[0:HALO] = winds[0:HALO].astype(F32)
     windf[HALO + rows :] = winds[HALO + rows :].astype(F32)
     for o in (0, rows):
@@ -256,21 +273,18 @@
         index = lax.rem(me + k, 2 * HALO)
         send_row(index + inner * (index // HALO))
 
-    incoming[me] = done[me]
+    codes_in[me] = codes[me]
+    tops_in[me] = tops[me]
     for source in range(wide):
         @pl.when(source != me)
         def _():
-            pltpu.make_async_remote_copy(
-                src_ref=done.at[source],
-                dst_ref=incoming.at[source],
-                send_sem=row_send.at[source],
-                recv_sem=row_recv.at[source],
-                device_id={"wide": source},
-                device_id_type=MESH,
-            ).wait_recv()
+            for copy in row_copies(source, source):
+                copy.wait_recv()
 
     for source in range(wide):
-        cells[source * groups : (source + 1) * groups] = incoming[source]
+        cells[source * groups : (source + 1) * groups] = (
+            from_codes(codes_in[source]) * tops_in[source]
+        )
 
     block = species
 
@@ -303,7 +317,8 @@
     for row in range(rows):
         @pl.when(row != me)
         def _():
-            row_copy(row).wait_send()
+            for copy in row_copies(row, me):
+                copy.wait_send()
 
 
 def on_device(wide, concentrations, wind_speeds, rate_constants, reactants, products):
@@ -326,10 +341,14 @@
             pltpu.VMEM((2, reactions), jnp.int32),
             pltpu.VMEM((rows + 2 * HALO, groups, columns), F32),
             pltpu.VMEM((rows + HALO, groups, columns), F32),
-            pltpu.VMEM((rows, groups, columns), F32),
+            pltpu.VMEM((2, HALO, groups, columns), jnp.int16),
+            pltpu.VMEM((2, HALO, groups, columns), jnp.int16),
+            pltpu.VMEM((rows, groups, columns), jnp.int16),
+            pltpu.VMEM((rows, 1, columns), F32),
             pltpu.VMEM((rows + 2 * HALO, 2, 2, columns), BF16),
             pltpu.VMEM((rows + 2 * HALO, 2, 2, columns), F32),
-            pltpu.VMEM((wide, groups, columns), F32),
+            pltpu.VMEM((wide, groups, columns), jnp.int16),
+            pltpu.VMEM((wide, 1, columns), F32),
             pltpu.VMEM((species, columns), F32),
             pltpu.VMEM((species, columns), F32),
             pltpu.VMEM((2, reactions, species), BF16),
@@ -338,7 +357,7 @@
             pltpu.VMEM((reactions, columns), BF16),
             pltpu.VMEM((reactions, columns), F32),
             dma((wide,)), dma((rows + 2 * HALO,)), dma((2, wide)),
-            dma((2,)), dma((2,)), dma((rows,)), dma((wide,)), dma((5,)),
+            dma((2,)), dma((2,)), dma((2, rows)), dma((2, wide)), dma((5,)),
         ],
         compiler_params=pltpu.CompilerParams(collective_id=0, has_side_effects=True),
         name="transport_chemistry",

time: 28.1 us -> 26.2 us (0.932)
  Pallas kernels: 26.1 us -> 24.2 us
    pallas_call x1, Pallas kernels: 26.1 us -> 24.2 us  [on_device(): pl.pallas_call(kernel, out_shape=jax.ShapeDtypeStruct((species * columns...]
where the time goes in v3:
time: 26.2 us; the launch traced here: 26 us
  Pallas kernels  24.2 us (92%)
  local copies, waits for them, and re-layouts  1.83 us (7%)
    pallas_call x1, Pallas kernels, on_device(): pl.pallas_call(kernel, out_shape=jax.ShapeDtypeStruct((species * columns...  24.2 us
    unnamed x1, local copies, waits for them, and re-layouts  1.83 us

profile of v3, /device:TPU:0, one launch (start us, length us, event | category | flops | bytes accessed | tf_op | source)
XLA Modules:
  0.0 26.0 jit_solution(10177943443099881361)
XLA Ops:
  0.0 24.2 %transport_chemistry.1 = f32[512,128]{1,0:T(8,128)} custom-call(f32[16,16,256]{2,1,0:T(8,128)} %conc_in.1, bf16[2,2,256]{2,1,0:T(2,128)(2,1)} %bitcast.9, f32[6,128]{1,0:T(8,128)} %bitcast.8, s32[2,768]{1,0:T(2,128)} %bitcast.6, s32[2,768]{1,0:T(2,128)} %bitcast.7), custom_call_target="tpu_custom_call" | custom-call | tf_op jit(solution)/shard_map/transport_chemistry/pallas_call | solution.py:332
  24.2 1.8 %copy.8 = f32[256,1,256]{2,1,0:T(1,128)} copy(f32[256,1,256]{2,1,0:T(1,128)} %bitcast.5) | data formatting | bytes 524288

commit v4 on v3

--- a/solution.py
+++ b/solution.py
@@ -68,7 +68,7 @@
 
 
 def kernel(
-    conc_in, wind_ref, k_in, react_in, prod_in, out_ref,
+    conc_in, wind_in, k_in, react_in, prod_in, out_ref,
     conc_ref, k_ref, react_ref, prod_ref,
     ext, mid, rims_out, rims_in, codes, tops, winds, windf, codes_in, tops_in, cells, cells_left, picks, net, gain, rates, rates_left,
     wind_send, wind_recv, rim_send, halo_send, halo_recv, row_send, row_recv, load_sem,
@@ -111,11 +111,11 @@
                 (react_in, react_ref),
                 (prod_in, prod_ref),
                 (k_in, k_ref),
-                (wind_ref, winds.at[HALO + me]),
+                (wind_in, winds.at[HALO + me]),
             )
         )
     ]
-    for copy in loads:
+    for copy in loads[::-1]:
         copy.start()
 
     low_rim = (wide - 1 - me + HALO) // wide
@@ -124,7 +124,7 @@
 
     def wind_copy(slot, send, **device):
         return pltpu.make_async_remote_copy(
-            src_ref=wind_ref,
+            src_ref=winds.at[HALO + me],
             dst_ref=winds.at[slot],
             send_sem=send,
             recv_sem=wind_recv.at[slot],
@@ -174,6 +174,7 @@
         for side, other in enumerate((above, below))
     ]
 
+    loads[-1].wait()
     for copy in wind_copies:
         copy.start()
     rim_copies(lambda copy: copy.start())
@@ -186,7 +187,7 @@
     for copy in halos:
         copy.start()
 
-    for copy in loads[1:]:
+    for copy in loads[1:-1]:
         copy.wait()
     ids = lax.broadcasted_iota(jnp.int32, (species, reactions), 0)
 
@@ -208,10 +209,8 @@
     def wind_arrival(slot):
         wind_copy(slot, wind_send.at[0], wide=lax.rem(me + 1, wide)).wait_recv()
 
-    for source in range(wide):
-        @pl.when(source != me)
-        def _():
-            wind_arrival(HALO + source)
+    for step in range(1, wide):
+        wind_arrival(HALO + lax.rem(me + step, wide))
 
     windf[HALO : HALO + rows] = winds[HALO : HALO + rows].astype(F32)
 
@@ -242,19 +241,12 @@
             for index, (here, there) in enumerate(((codes, codes_in), (tops, tops_in)))
         ]
 
-    def send_row(row):
-        @pl.when(row != me)
-        def _():
-            for copy in row_copies(row, me):
-                copy.start()
-
-    inner = rows - 2 * HALO
+    others = [lax.rem(me + step, wide) for step in range(1, wide)]
+
     for o in range(HALO, rows, CHUNK):
         first_substep(o)
     for g in range(HALO, rows - HALO, CHUNK):
         second_substep(g)
-    for k in range(inner):
-        send_row(HALO + lax.rem(me + k, inner))
 
     for slot in range(HALO):
         wind_arrival(slot)
@@ -269,17 +261,14 @@
         first_substep(o)
     for g in (0, rows - HALO):
         second_substep(g)
-    for k in range(2 * HALO):
-        index = lax.rem(me + k, 2 * HALO)
-        send_row(index + inner * (index // HALO))
-
+    for other in others:
+        for copy in row_copies(other, me):
+            copy.start()
     codes_in[me] = codes[me]
     tops_in[me] = tops[me]
-    for source in range(wide):
-        @pl.when(source != me)
-        def _():
-            for copy in row_copies(source, source):
-                copy.wait_recv()
+    for other in others:
+        for copy in row_copies(other, other):
+            copy.wait_recv()
 
     for source in range(wide):
         cells[source * groups : (source + 1) * groups] = (
@@ -314,11 +303,15 @@
     rim_copies(lambda copy: copy.wait_send())
     for copy in halos:
         copy.wait_send()
-    for row in range(rows):
-        @pl.when(row != me)
-        def _():
-            for copy in row_copies(row, me):
-                copy.wait_send()
+    for other in others:
+        for copy in row_copies(other, me):
+            copy.wait_send()
+
+
+def place_kernel(result_ref, out_ref, sem):
+    copy = pltpu.make_async_copy(result_ref, out_ref, sem)
+    copy.start()
+    copy.wait()
 
 
 def on_device(wide, concentrations, wind_speeds, rate_constants, reactants, products):
@@ -329,10 +322,17 @@
     wind = jnp.swapaxes(wind_speeds, 1, 2).reshape(2, 2, columns)
     lanes = 128
     dma = pltpu.SemaphoreType.DMA
+    inputs = (
+        concentrations,
+        wind,
+        rate_constants.reshape(-1, lanes),
+        reactants.T,
+        products.T,
+    )
     result = pl.pallas_call(
         kernel,
         out_shape=jax.ShapeDtypeStruct((species * columns // lanes, lanes), F32),
-        in_specs=[pl.BlockSpec(memory_space=pl.ANY)] * 5,
+        in_specs=[pl.BlockSpec(memory_space=pltpu.HBM)] * 5,
         out_specs=pl.BlockSpec(memory_space=pltpu.VMEM),
         scratch_shapes=[
             pltpu.VMEM((groups, rows, columns), F32),
@@ -359,9 +359,20 @@
             dma((wide,)), dma((rows + 2 * HALO,)), dma((2, wide)),
             dma((2,)), dma((2,)), dma((2, rows)), dma((2, wide)), dma((5,)),
         ],
-        compiler_params=pltpu.CompilerParams(collective_id=0, has_side_effects=True),
+        compiler_params=pltpu.CompilerParams(
+            collective_id=0, has_side_effects=True, vmem_limit_bytes=24 * 2**20
+        ),
         name="transport_chemistry",
-    )(concentrations, wind, rate_constants.reshape(-1, lanes), reactants.T, products.T)
+    )(*[pltpu.with_memory_space_constraint(each, pltpu.HBM) for each in inputs])
+    result = pl.pallas_call(
+        place_kernel,
+        out_shape=jax.ShapeDtypeStruct(result.shape, F32),
+        in_specs=[pl.BlockSpec(memory_space=pltpu.VMEM)],
+        out_specs=pl.BlockSpec(memory_space=pl.ANY),
+        scratch_shapes=[dma(())],
+        compiler_params=pltpu.CompilerParams(vmem_limit_bytes=2**20),
+        name="place",
+    )(result)
     return result.reshape(species, 1, columns)
 
 

time: 26.2 us -> 23.4 us (0.89)
  local copies, waits for them, and re-layouts: 1.83 us -> 0 us
  Pallas kernels: 24.2 us -> 23.3 us
    unnamed x1 -> x0, local copies, waits for them, and re-layouts: 1.83 us -> none
    pallas_call x1, Pallas kernels: 24.2 us -> 22.6 us  [on_device(): pl.pallas_call(kernel, out_shape=jax.ShapeDtypeStruct((species * columns...]
    pallas_call x0 -> x1, Pallas kernels: none -> 0.71 us  [on_device(): pl.pallas_call(place_kernel, out_shape=jax.ShapeDtypeStruct(result.shape,...]
where the time goes in v4:
time: 23.4 us; the launch traced here: 23.3 us
  Pallas kernels  23.3 us (100%)
    pallas_call x1, Pallas kernels, on_device(): pl.pallas_call(kernel, out_shape=jax.ShapeDtypeStruct((species * columns...  22.6 us
    pallas_call x1, Pallas kernels, on_device(): pl.pallas_call(place_kernel, out_shape=jax.ShapeDtypeStruct(result.shape,...  0.71 us

profile of v4, /device:TPU:0, one launch (start us, length us, event | category | flops | bytes accessed | tf_op | source)
XLA Modules:
  0.0 23.3 jit_solution(6658685653774808777)
XLA Ops:
  0.0 22.6 %transport_chemistry.1.result_ref = f32[512,128]{1,0:T(8,128)S(1)} custom-call(f32[16,16,256]{2,1,0:T(8,128)} %conc_in.1, bf16[2,2,256]{2,1,0:T(2,128)(2,1)} %bitcast.8, f32[6,128]{1,0:T(8,128)} %bitcast.7, s32[2,768]{1,0:T(2,128)} %bitcast.5, s32[2,768]{1,0:T(2,128)} %bitcast.6), custom_call_target="tpu_custom_call" | custom-call | tf_op jit(solution)/shard_map/transport_chemistry/pallas_call | solution.py:332
  22.6 0.7 %place.1 = f32[512,128]{1,0:T(8,128)} custom-call(f32[512,128]{1,0:T(8,128)S(1)} %transport_chemistry.1.result_ref), custom_call_target="tpu_custom_call" | custom-call | tf_op jit(solution)/shard_map/place/pallas_call | solution.py:367

commit v5 on v4

--- a/solution.py
+++ b/solution.py
@@ -262,7 +262,7 @@
     for g in (0, rows - HALO):
         second_substep(g)
     for other in others:
-        for copy in row_copies(other, me):
+        for copy in row_copies(other, me)[::-1]:
             copy.start()
     codes_in[me] = codes[me]
     tops_in[me] = tops[me]
@@ -293,7 +293,7 @@
         cells[...] = q + jnp.dot(net[...], rates[...], preferred_element_type=F32)
         return carry
 
-    lax.fori_loop(0, SECTIONS, section, 0)
+    lax.fori_loop(0, SECTIONS, section, 0, unroll=True)
     parts = columns // lanes
     for part in range(parts):
         out_ref[pl.ds(part, species, stride=parts), :] = cells[:, part * lanes : (part + 1) * lanes]

time: 23.4 us -> 23.1 us (0.987)
  Pallas kernels: 23.3 us -> 23 us
    pallas_call x1, Pallas kernels: 22.6 us -> 22.3 us  [on_device(): pl.pallas_call(kernel, out_shape=jax.ShapeDtypeStruct((species * columns...]
where the time goes in v5:
time: 23.1 us; the launch traced here: 23 us
  Pallas kernels  23 us (100%)
    pallas_call x1, Pallas kernels, on_device(): pl.pallas_call(kernel, out_shape=jax.ShapeDtypeStruct((species * columns...  22.3 us
    pallas_call x1, Pallas kernels, on_device(): pl.pallas_call(place_kernel, out_shape=jax.ShapeDtypeStruct(result.shape,...  0.71 us

profile of v5, /device:TPU:0, one launch (start us, length us, event | category | flops | bytes accessed | tf_op | source)
XLA Modules:
  0.0 23.0 jit_solution(15736725942630041239)
XLA Ops:
  0.0 22.3 %transport_chemistry.1.result_ref = f32[512,128]{1,0:T(8,128)S(1)} custom-call(f32[16,16,256]{2,1,0:T(8,128)} %conc_in.1, bf16[2,2,256]{2,1,0:T(2,128)(2,1)} %bitcast.8, f32[6,128]{1,0:T(8,128)} %bitcast.7, s32[2,768]{1,0:T(2,128)} %bitcast.5, s32[2,768]{1,0:T(2,128)} %bitcast.6), custom_call_target="tpu_custom_call" | custom-call | tf_op jit(solution)/shard_map/transport_chemistry/pallas_call | solution.py:332
  22.3 0.7 %place.1 = f32[512,128]{1,0:T(8,128)} custom-call(f32[512,128]{1,0:T(8,128)S(1)} %transport_chemistry.1.result_ref), custom_call_target="tpu_custom_call" | custom-call | tf_op jit(solution)/shard_map/place/pallas_call | solution.py:367
